TPU v7x, 256 devices: a whole 4x4x8 slice. The times are simulated.
256 devices in a mesh: feat: 32 (over x_lo, z, core), tok: 8 (over x_hi, y).
Axes of the slice: x: 4 (x_hi: 2, x_lo: 2; x = x_hi * 2 + x_lo), y: 4, z: 8, core: 2. Of those that a mesh axis runs over, the one named last changes fastest.
Arguments:
- acts_in: bfloat16 [3072, 2, 2304], P(('tok', 'feat')), may hold values from -6 to 6
- targets: bfloat16 [3072, 2, 2304], P(('tok', 'feat')), may hold values from -6 to 6
- enc_weight: bfloat16 [2, 2304, 16384], P(None, None, 'feat'), may hold values from -0.125 to 0.125
- enc_bias: float32 [2, 16384], P(None, 'feat'), may hold values from -3 to 3
- dec_weight: bfloat16 [3, 16384, 2304], P(None, 'feat'), may hold values from -0.046875 to 0.046875
Outputs:
- grad_enc: bfloat16 [2, 2304, 16384], P(None, 'tok', 'feat')
- grad_enc_bias: float32 [2, 16384], P(None, ('feat', 'tok'))
- grad_dec: bfloat16 [3, 16384, 2304], P(None, ('feat', 'tok'))
All inputs are finite; a program needn't handle non-finite values.
Results may differ from a plain program's by a relative error of at most 0.02.
Values may be sent and summed in bfloat16 or wider, within the bound.
A program may use at most 128 MiB of HBM per device.

v0:
```python
import math

import jax
import jax.numpy as jnp
from jax import lax
from jax.sharding import PartitionSpec as P


def pair_slot(source, target, layers):
    return sum((layers - k for k in range(source))) + (target - source)


def shards(acts_in, targets, enc_weight, enc_bias, dec_weight):
    layers = enc_weight.shape[0]
    inputs, wanted = (
        lax.all_gather(acts_in, "feat", axis=0, tiled=True),
        lax.all_gather(targets, "feat", axis=0, tiled=True),
    )
    tok_rows = inputs.shape[0]
    loss_scale = 1.0 / math.sqrt(tok_rows * lax.axis_size("tok"))
    preacts = []
    coded = []
    for source in range(layers):
        value = (
            jnp.dot(inputs[:, source, :], enc_weight[source], preferred_element_type=jnp.float32)
            + enc_bias[source]
        )
        preacts.append(value)
        coded.append((0.5 * jnp.maximum(value, 0.0) ** 2).astype(jnp.bfloat16))
    pieces = [code for code in coded]
    rebuilt = []
    for decode_target in range(layers):
        total = jnp.dot(
            pieces[0],
            dec_weight[pair_slot(0, decode_target, layers)],
            preferred_element_type=jnp.float32,
        )
        for decode_source in range(1, decode_target + 1):
            total = total + jnp.dot(
                pieces[decode_source],
                dec_weight[pair_slot(decode_source, decode_target, layers)],
                preferred_element_type=jnp.float32,
            )
        rebuilt.append(total)
    summed = lax.psum(jnp.stack(rebuilt, axis=1).astype(jnp.bfloat16), "feat").astype(jnp.float32)
    errors = (summed - wanted.astype(jnp.float32)).astype(jnp.bfloat16)
    dec_parts = []
    for source in range(layers):
        for target in range(source, layers):
            dec_parts.append(
                lax.dot_general(
                    coded[source],
                    errors[:, target, :],
                    (((0,), (0,)), ((), ())),
                    preferred_element_type=jnp.float32,
                )
                * loss_scale
            )
    dec_terms = jnp.stack(dec_parts)
    enc_parts = []
    bias_parts = []
    for source in range(layers):
        dcoded = lax.dot_general(
            errors[:, source, :],
            dec_weight[pair_slot(source, source, layers)],
            (((1,), (1,)), ((), ())),
            preferred_element_type=jnp.float32,
        )
        for target in range(source + 1, layers):
            dcoded = dcoded + lax.dot_general(
                errors[:, target, :],
                dec_weight[pair_slot(source, target, layers)],
                (((1,), (1,)), ((), ())),
                preferred_element_type=jnp.float32,
            )
        dpreact = (dcoded * jnp.maximum(preacts[source], 0.0)).astype(jnp.bfloat16)
        enc_parts.append(
            lax.dot_general(
                inputs[:, source, :],
                dpreact,
                (((0,), (0,)), ((), ())),
                preferred_element_type=jnp.float32,
            )
            * loss_scale
        )
        bias_parts.append(jnp.sum(dpreact.astype(jnp.float32), axis=0) * loss_scale)
    enc_terms = jnp.stack(enc_parts)
    bias_terms = jnp.stack(bias_parts)
    enc_summed, bias_summed, dec_summed = (
        lax.psum_scatter(
            enc_terms.astype(jnp.bfloat16), "tok", scatter_dimension=1, tiled=True
        ).astype(jnp.float32),
        lax.psum_scatter(
            bias_terms.astype(jnp.bfloat16), "tok", scatter_dimension=1, tiled=True
        ).astype(jnp.float32),
        lax.psum_scatter(
            dec_terms.astype(jnp.bfloat16), "tok", scatter_dimension=1, tiled=True
        ).astype(jnp.float32),
    )
    return (enc_summed.astype(jnp.bfloat16), bias_summed, dec_summed.astype(jnp.bfloat16))


def solution(mesh):
    return jax.shard_map(
        shards,
        mesh=mesh,
        in_specs=(
            P(("tok", "feat"), None, None),
            P(("tok", "feat"), None, None),
            P(None, None, "feat"),
            P(None, "feat"),
            P(None, "feat", None),
        ),
        out_specs=(
            P(None, "tok", "feat"),
            P(None, ("feat", "tok")),
            P(None, ("feat", "tok"), None),
        ),
        check_vma=False,
    )
```

profile of v0, /device:TPU:1, one launch (start us, length us, event | category | flops | bytes accessed | tf_op | source)
XLA Modules:
  0.0 719.0 jit_solution(3536955893917126008)
XLA Ops:
  8.7 0.8 fusion.65
  9.5 70.8 %all-gather.3.cloned.1.call-done = bf16[384,2,2304]{2,1,0:T(2,128)(2,1)} async-done(((bf16[12,2,2304]{2,1,0:T(2,128)(2,1)}), bf16[384,2,2304]{2,1,0:T(2,128)(2,1)}) %all-gather.3.cloned.1.call-update) | async-done | bytes 3538960 | tf_op jit(solution)/shard_map/all_gather | solution.py:16
  80.3 7.9 %fusion.64 = (bf16[384,1,2304]{2,1,0:T(2,128)(2,1)S(1)}, bf16[384,1,2304]{2,1,0:T(2,128)(2,1)S(1)}) fusion(bf16[384,2,2304]{2,1,0:T(2,128)(2,1)} %all-gather.3.cloned.1.call-done), kind=kLoop, calls=%fused_computation.69 | loop fusion | bytes 7077888 | tf_op jit(solution)/shard_map/slice | solution.py:79
  88.3 5.0 multiply_convert_fusion.1
  93.2 1.1 fusion.11
  94.3 1.1 fusion.20
  95.5 1.1 fusion.53
  96.6 0.9 copy-done.5
  97.4 1.1 fusion.12
  98.6 2.2 pad_maximum_fusion.2
  100.8 47.1 %all-gather.5.cloned.1.call-done = bf16[384,2,2304]{2,1,0:T(2,128)(2,1)} async-done(((bf16[12,2,2304]{2,1,0:T(2,128)(2,1)}), bf16[384,2,2304]{2,1,0:T(2,128)(2,1)}) %all-gather.5.cloned.1.call-update) | async-done | bytes 3538960 | tf_op jit(solution)/shard_map/all_gather | solution.py:17
  147.9 233.3 %all-reduce.4.cloned.1.call-done = bf16[384,2,2304]{2,0,1:T(8,128)(2,1)} async-done(((bf16[384,2,2304]{2,0,1:T(8,128)(2,1)}), bf16[384,2,2304]{2,0,1:T(8,128)(2,1)}) %all-reduce.4.cloned.1.call-update) | async-done | bytes 3538960 | tf_op jit(solution)/shard_map/psum | solution.py:45
  381.3 4.0 subtract_convert_fusion
  385.3 4.1 convert_reduce_fusion
  389.4 2.9 fusion.18
  392.3 2.9 fusion.9
  395.2 2.8 convert_reduce_fusion.1
  398.0 2.9 fusion.10
  401.0 0.8 copy.18
  402.0 4.9 pad_maximum_fusion.1
  407.0 12.4 %copy.16 = bf16[2,2304,512]{2,0,1:T(2,128)(2,1)} copy(bf16[2,2304,512]{1,2,0:T(8,128)(2,1)} %pad_maximum_fusion.1) | data formatting | bytes 9437184 | tf_op jit(solution)/shard_map/stack | solution.py:87
  419.4 1.9 copy-done.3
  421.3 2.5 fusion.7
  423.9 1.4 fusion.8
  425.3 1.4 fusion.6
  426.7 3.5 pad_maximum_fusion
  432.2 43.0 %reduce-scatter.7.cloned.1.call-done = bf16[64,2]{1,0:T(8,128)(2,1)} async-done(((bf16[512,2]{1,0:T(8,128)(2,1)}), bf16[64,2]{1,0:T(8,128)(2,1)}) %reduce-scatter.7.cloned.1.call-update) | async-done | bytes 272
  475.2 0.8 copy.19
  476.5 124.8 %all-reduce.6.cloned.1.call-done = bf16[2,2304,512]{2,0,1:T(2,128)(2,1)} async-done(((bf16[2,2304,512]{2,0,1:T(2,128)(2,1)}), bf16[2,2304,512]{2,0,1:T(2,128)(2,1)}) %all-reduce.6.cloned.1.call-update) | async-done | bytes 4718608
  601.3 1.5 constant_dynamic-slice_fusion
  602.8 0.9 copy.17
  603.7 108.5 %reduce-scatter.5.cloned.1.call-done = bf16[3,64,2304]{2,1,0:T(8,128)(2,1)} async-done(((bf16[3,512,2304]{2,1,0:T(8,128)(2,1)}), bf16[3,64,2304]{2,1,0:T(8,128)(2,1)}) %reduce-scatter.5.cloned.1.call-update) | async-done | bytes 884752 | tf_op jit(solution)/shard_map/reduce_scatter | solution.py:96
  (46 shorter events, 3.8 us)
Async XLA Ops:
  7.2 73.1 %all-gather.3.cloned.1.call-start = ((), (), s32[]{:S(2)}) async-start(), calls=%async_computation.2 | async-start | bytes 3649536 | tf_op jit(solution)/shard_map/all_gather | solution.py:16
  7.9 140.0 %all-gather.5.cloned.1.call-start = ((), (), s32[]{:S(2)}) async-start(), calls=%async_computation.4 | async-start | bytes 3649536 | tf_op jit(solution)/shard_map/all_gather | solution.py:17
  8.6 372.6 %all-reduce.4.cloned.1.call-start = ((), (), s32[]{:S(2)}) async-start(), calls=%async_computation.3 | async-start | bytes 7077888 | tf_op jit(solution)/shard_map/psum | solution.py:45
  88.2 7.2 %copy-start = (bf16[384,1,2304]{2,1,0:T(2,128)(2,1)}, bf16[384,1,2304]{2,1,0:T(2,128)(2,1)S(1)}, u32[]{:S(2)}) copy-start(bf16[384,1,2304]{2,1,0:T(2,128)(2,1)S(1)} %get-tuple-element.13) | copy-start | bytes 5308420
  88.2 5.0 copy-start.4
  88.2 7.2 %slice-start = ((s8[4718592]{0:T(1024)(128)(4,1)}), s8[4194304]{0:T(1024)(128)(4,1)S(1)}, s32[]{:S(2)}) async-start(s8[4718592]{0:T(1024)(128)(4,1)} %bitcast.108), calls=%async_computation.8 | async-start | bytes 8388608
  93.2 2.2 copy-start.8
  93.2 2.2 slice-start.1
  96.6 0.9 copy-start.5
  100.8 374.4 %reduce-scatter.7.cloned.1.call-start = ((), (), s32[]{:S(2)}) async-start(), calls=%async_computation.6 | async-start | bytes 147456
  381.3 4.0 copy-start.6
  385.3 9.9 %copy-start.2 = (bf16[384,2,2304]{2,0,1:T(8,128)(2,1)}, bf16[384,2,2304]{2,0,1:T(8,128)(2,1)S(1)}, u32[]{:S(2)}) copy-start(bf16[384,2,2304]{2,0,1:T(8,128)(2,1)S(1)} %subtract_convert_fusion) | copy-start | bytes 10616836
  389.4 2.9 copy-start.1
  392.3 2.9 copy-start.11
  401.8 199.5 %all-reduce.6.cloned.1.call-start = ((), (), s32[]{:S(2)}) async-start(), calls=%async_computation.7 | async-start | bytes 9437184
  419.3 2.0 copy-start.3
  419.4 292.8 %reduce-scatter.5.cloned.1.call-start = ((), (), s32[]{:S(2)}) async-start(), calls=%async_computation.5 | async-start | bytes 7962624 | tf_op jit(solution)/shard_map/reduce_scatter | solution.py:96
  421.3 2.5 copy-start.9
  423.8 1.4 copy-start.7
  430.3 0.7 copy-start.10
Sparse Core Ops, SparseCore 0:
  9.8 70.3 all-gather.2
  82.1 65.7 all-gather.4
  150.6 230.6 all-reduce.3
  401.9 73.2 reduce-scatter.6
  477.7 123.5 all-reduce.5
  606.0 106.1 reduce-scatter.4
where the time goes:
time: 720 us; the launch traced here: 719 us
  waiting for transfers between devices  629 us (87%)
  matrix products  30.2 us (4%)
  local copies, waits for them, and re-layouts  29.1 us (4%)
  other arithmetic  15.2 us (2%)
  between operations  15 us (2%)
    psum x1, waiting for transfers between devices, shards(): lax.psum(jnp.stack(rebuilt, axis=1).astype(jnp.bfloat16), 'feat')  233 us
    unnamed x8, waiting for transfers between devices  169 us
    reduce_scatter x1, waiting for transfers between devices, shards(): lax.psum_scatter(dec_terms.astype(jnp.bfloat16), 'tok', scatter_dimension...  108 us
    all_gather x1, waiting for transfers between devices, shards(): lax.all_gather(acts_in, 'feat', axis=0, tiled=True)  70.8 us
    all_gather x1, waiting for transfers between devices, shards(): lax.all_gather(targets, 'feat', axis=0, tiled=True)  47.1 us
  transfers between devices with their start and end apart: 6, of which 6 were waited for; matrix products, arithmetic and copies ran while one was open for 7% of the time, Pallas kernels for 0%

commit v1 on v0

v1 whole, which is shorter than its diff:
```python
import math

import jax
import jax.numpy as jnp
from jax import lax
from jax.experimental import pallas as pl
from jax.experimental.pallas import tpu as pltpu
from jax.sharding import PartitionSpec as P

MESH = pl.DeviceIdType.MESH
F32 = jnp.float32
BF16 = jnp.bfloat16
XN, ZN, YN = 4, 8, 4
TD = 12
ROWS = XN * TD
COLS = 1152
FH = 256
AG_ORDER = (0, -1, 1, -2, 2, -3, 3, 4)
RS_ORDER = (4, 3, -3, 2, -2, 1, -1, 0)
PAIR = {(0, 0): 0, (0, 1): 1, (1, 1): 2}


def kernel(inp, eb, ew_hbm, dw_hbm, ge_out, gb_out, gd_out,
           land, acts, tgt, errs, ew, dw, gate, coded, coded_t, dpre, part, sib, recv,
           gdec, genc, rone_d, rone_e, rtwo_d, rtwo_e, swap, bsum, bland,
           wsem, a2a_s, a2a_r, ag1_s, ag1_r, rs_s, rs_r, ag2_s, ag2_r, y_s, y_r, b_s, b_r, sw_s, sw_r):
    fi = lax.axis_index("feat")
    ti = lax.axis_index("tok")
    core = fi % 2
    z = (fi // 2) % ZN
    xlo = fi // (2 * ZN)
    y = ti % YN
    xhi = ti // YN
    x = 2 * xhi + xlo
    scale = 1.0 / math.sqrt(3072.0)

    def dev(xx, zz, yy, cc):
        return ((xx % 2) * (2 * ZN) + zz * 2 + cc, (xx // 2) * YN + yy)

    def xd(d):
        return dev((x + d) % XN, z, y, core)

    def zd(d):
        return dev(x, (z + d + ZN) % ZN, y, core)

    def yd(d):
        return dev(x, z, (y + d) % YN, core)

    def zat(s):
        return (z + s + ZN) % ZN

    def xat(d):
        return (x + d) % XN

    sibling = dev(x, z, y, 1 - core)

    def rcopy(src, dst, ssem, rsem, device):
        return pltpu.make_async_remote_copy(src_ref=src, dst_ref=dst, send_sem=ssem, recv_sem=rsem, device_id=device, device_id_type=MESH)

    def got(dst, rsem):
        rcopy(dst, dst, rsem, rsem, sibling).wait_recv()

    fo = pl.multiple_of(xhi * FH, FH)
    w_copies = [pltpu.make_async_copy(ew_hbm.at[:, :, pl.ds(fo, FH)], ew, wsem.at[0]),
                pltpu.make_async_copy(dw_hbm.at[:, pl.ds(fo, FH), :], dw, wsem.at[1])]
    for copy in w_copies:
        copy.start()

    barrier = pltpu.get_barrier_semaphore()
    partners = [sibling] + [xd(d) for d in (1, 2, 3)] + [zd(1), zd(-1)] + [yd(d) for d in (1, 2, 3)]
    for partner in partners:
        pl.semaphore_signal(barrier, inc=1, device_id=partner, device_id_type=MESH)
    pl.semaphore_wait(barrier, len(partners))

    sends = []
    for d in (1, 2, 3):
        send = rcopy(inp.at[:, xat(d)], land.at[:, d], a2a_s.at[d], a2a_r.at[d], xd(d))
        send.start()
        sends.append(send)
    land[:, 0] = inp[:, x]
    row = lax.broadcasted_iota(jnp.int32, (ROWS, XN * 16), 0)
    col = lax.broadcasted_iota(jnp.int32, (ROWS, XN * 16), 1)
    source = (x + XN - col // 16) % XN
    place = jnp.where((row == TD * source + col % 16) & (col % 16 < TD), 1.0, 0.0).astype(BF16)
    for d in (1, 2, 3):
        got(land.at[:, d], a2a_r.at[d])
    acts[x, z, core] = jnp.dot(place, land[0].reshape(XN * 16, COLS), preferred_element_type=F32).astype(BF16)
    tgt[...] = jnp.dot(place, land[1].reshape(XN * 16, COLS), preferred_element_type=F32)

    def gather(buf, s_sem, r_sem):
        @pl.when(core == 0)
        def _():
            out = []

            def send(xx, zz, device, r):
                unit = buf.at[xx, zz, 0]
                one = rcopy(unit, unit, s_sem.at[len(out)], r_sem.at[r], device)
                one.start()
                out.append(one)

            def to_x(i):
                zz = zat(AG_ORDER[i])
                send(x, zz, xd(1), 8 + i)
                send(x, zz, xd(3), 16 + i)

            def from_x(i):
                zz = zat(AG_ORDER[i])
                got(buf.at[xat(3), zz, 0], r_sem.at[8 + i])
                if AG_ORDER[i] % 2 == 0:
                    send(xat(3), zz, xd(1), 24 + i)
                got(buf.at[xat(1), zz, 0], r_sem.at[16 + i])
                if AG_ORDER[i] % 2 == 1:
                    send(xat(1), zz, xd(3), 24 + i)

            def to_sibling(i):
                zz = zat(AG_ORDER[i])
                got(buf.at[xat(2), zz, 0], r_sem.at[24 + i])
                bundle = buf.at[:, zz, 0]
                one = rcopy(bundle, bundle, s_sem.at[len(out)], r_sem.at[32 + i], sibling)
                one.start()
                out.append(one)

            send(x, z, zd(1), AG_ORDER.index(-1))
            send(x, z, zd(-1), AG_ORDER.index(1))
            to_x(0)
            for i in range(1, 8):
                s = AG_ORDER[i]
                got(buf.at[x, zat(s), 0], r_sem.at[i])
                if s < 0:
                    send(x, zat(s), zd(1), AG_ORDER.index(s - 1 if s > -3 else 4))
                elif s < 3:
                    send(x, zat(s), zd(-1), AG_ORDER.index(s + 1))
                to_x(i)
                from_x(i - 1)
                if i > 1:
                    to_sibling(i - 2)
            from_x(7)
            to_sibling(6)
            to_sibling(7)
            for i in range(8):
                got(buf.at[:, zat(AG_ORDER[i]), 1], r_sem.at[32 + i])
            for one in out:
                one.wait_send()

        @pl.when(core == 1)
        def _():
            out = []

            def send(ref, device, r):
                one = rcopy(ref, ref, s_sem.at[len(out)], r_sem.at[r], device)
                one.start()
                out.append(one)

            for d in (1, 2, 3):
                send(buf.at[x, z, 1], xd(d), d)
            for d in (1, 2, 3):
                got(buf.at[xat(4 - d), z, 1], r_sem.at[d])
            send(buf.at[:, z, 1], zd(1), 8 + 1)
            send(buf.at[:, z, 1], zd(-1), 16 + 1)
            send(buf.at[:, z, 1], sibling, 32)
            for k in (1, 2, 3, 4):
                for sign in (-1, 1):
                    zz = zat(sign * k)
                    base = 8 if sign == -1 else 16
                    half = buf.at[0:2, zz, 1] if sign == -1 else buf.at[2:4, zz, 1]
                    bundle = buf.at[:, zz, 1]
                    got(bundle if k < 4 else half, r_sem.at[base + k])
                    if k < 4:
                        send(bundle if k < 3 else half, zd(-sign), base + k + 1)
                        send(bundle, sibling, 32 + AG_ORDER.index(sign * k))
            send(buf.at[:, zat(4), 1], sibling, 32 + 7)
            for i in range(8):
                got(buf.at[:, zat(AG_ORDER[i]), 0], r_sem.at[32 + i])
            for one in out:
                one.wait_send()

    gather(acts, ag1_s, ag1_r)
    for copy in w_copies:
        copy.wait()

    bias = jnp.where(xhi == 0, eb[:, :FH], eb[:, FH:])
    for s in range(2):
        for half in range(2):
            rows = slice(384 * half, 384 * half + 384)
            zs = slice(4 * half, 4 * half + 4)
            value = jnp.dot(acts[2 * s, zs].reshape(384, COLS), ew[s, :COLS], preferred_element_type=F32)
            value = value + jnp.dot(acts[2 * s + 1, zs].reshape(384, COLS), ew[s, COLS:], preferred_element_type=F32)
            active = jnp.maximum(value + bias[s:s + 1], 0.0)
            gate[s, rows] = active
            code = (0.5 * active * active).astype(BF16)
            coded[s, rows] = code
            coded_t[s, :, rows] = code.T

    for t in range(2):
        for h in range(2):
            cols = slice(COLS * h, COLS * h + COLS)
            for quarter in range(4):
                rows = slice(192 * quarter, 192 * quarter + 192)
                total = jnp.dot(coded[0, rows], dw[PAIR[0, t], :, cols], preferred_element_type=F32)
                if t == 1:
                    total = total + jnp.dot(coded[1, rows], dw[PAIR[1, 1], :, cols], preferred_element_type=F32)
                part[2 * t + h, 2 * quarter:2 * quarter + 2] = total.astype(BF16).reshape(2, 2, ROWS, COLS)

    sib_sends = []
    for i, s in enumerate(RS_ORDER):
        one = rcopy(part.at[:, zat(s), 1 - core], sib.at[:, zat(s)], rs_s.at[40 + i], rs_r.at[40 + i], sibling)
        one.start()
        sib_sends.append(one)

    def add(dst, terms):
        def some(r, carry):
            sl = pl.ds(pl.multiple_of(r * 16, 16), 16)
            total = terms[0][sl, :].astype(F32)
            for term in terms[1:]:
                total = total + term[sl, :].astype(F32)
            dst[sl, :] = total.astype(dst.dtype)
            return carry

        lax.fori_loop(0, ROWS // 16, some, 0)

    def finish(terms):
        def some(r, carry):
            sl = pl.ds(pl.multiple_of(r * 16, 16), 16)
            total = terms[0][sl, :].astype(F32)
            for term in terms[1:]:
                total = total + term[sl, :].astype(F32)
            errs[x, z, core, sl, :] = (total - tgt[sl, :]).astype(BF16)
            return carry

        lax.fori_loop(0, ROWS // 16, some, 0)

    @pl.when(core == 0)
    def _():
        out = []

        def send(src, r, device):
            one = rcopy(src, recv.at[r], rs_s.at[len(out)], rs_r.at[r], device)
            one.start()
            out.append(one)

        for i, s in enumerate(RS_ORDER):
            zz = zat(s)
            got(sib.at[:, zz], rs_r.at[40 + i])
            unit = part.at[xat(2), zz, 0]
            add(unit, [unit, sib.at[xat(2), zz]])
            send(unit, i, xd(1) if s % 2 == 0 else xd(3))
        for i, s in enumerate(RS_ORDER):
            zz = zat(s)
            got(recv.at[i], rs_r.at[i])
            for d, base, parity in ((1, 8, 0), (3, 16, 1)):
                unit = part.at[xat(d), zz, 0]
                terms = [unit, sib.at[xat(d), zz]]
                if s % 2 == parity:
                    terms.append(recv.at[i])
                add(unit, terms)
                send(unit, base + i, xd(d))
        for i, s in enumerate(RS_ORDER):
            zz = zat(s)
            unit = part.at[x, zz, 0]
            terms = [unit, sib.at[x, zz]]
            got(recv.at[8 + i], rs_r.at[8 + i])
            got(recv.at[16 + i], rs_r.at[16 + i])
            terms += [recv.at[8 + i], recv.at[16 + i]]
            if 0 <= s < 4:
                got(recv.at[24 + (3 - s)], rs_r.at[24 + (3 - s)])
                terms.append(recv.at[24 + (3 - s)])
            if -3 < s <= 0:
                got(recv.at[28 + (2 + s)], rs_r.at[28 + (2 + s)])
                terms.append(recv.at[28 + (2 + s)])
            if s == 0:
                finish(terms)
            else:
                add(unit, terms)
                if s > 0:
                    send(unit, 24 + (4 - s), zd(1))
                else:
                    send(unit, 28 + (3 + s), zd(-1))
        for one in out:
            one.wait_send()

    @pl.when(core == 1)
    def _():
        out = []
        for i, s in enumerate(RS_ORDER):
            zz = zat(s)
            k = abs(s)
            got(sib.at[:, zz], rs_r.at[40 + i])
            up = down = 0
            if 0 <= s < 4:
                up = k + 1
                count = 2 if up == 4 else 4
                got(recv.at[4 * k:4 * k + count], rs_r.at[up])
            if -4 < s <= 0:
                down = k + 1
                count = 2 if down == 4 else 4
                got(recv.at[16 + 4 * k:16 + 4 * k + count], rs_r.at[8 + down])
            for xx in range(4):
                unit = part.at[xx, zz, 1]
                terms = [unit, sib.at[xx, zz]]
                if up and (up < 4 or xx < 2):
                    terms.append(recv.at[4 * k + xx])
                if down and (down < 4 or xx >= 2):
                    terms.append(recv.at[16 + 4 * k + (xx - 2 if down == 4 else xx)])
                add(unit, terms)
            hops = []
            if s == 4:
                hops = [(part.at[0:2, zz, 1], recv.at[12:14], 4, zd(1)), (part.at[2:4, zz, 1], recv.at[28:30], 12, zd(-1))]
            elif s > 0:
                hops = [(part.at[:, zz, 1], recv.at[4 * (k - 1):4 * k], k, zd(1))]
            elif s < 0:
                hops = [(part.at[:, zz, 1], recv.at[16 + 4 * (k - 1):16 + 4 * k], 8 + k, zd(-1))]
            for src, dst, r, device in hops:
                one = rcopy(src, dst, rs_s.at[len(out)], rs_r.at[r], device)
                one.start()
                out.append(one)
        for d in (1, 2, 3):
            one = rcopy(part.at[xat(d), z, 1], recv.at[32 + d], rs_s.at[len(out)], rs_r.at[16 + d], xd(d))
            one.start()
            out.append(one)
        for d in (1, 2, 3):
            got(recv.at[32 + d], rs_r.at[16 + d])
        finish([part.at[x, z, 1], recv.at[33], recv.at[34], recv.at[35]])
        for one in out:
            one.wait_send()

    for one in sib_sends:
        one.wait_send()

    gather(errs, ag2_s, ag2_r)

    y_sends = []

    def start(src, dst, n, d):
        one = rcopy(src, dst, y_s.at[n], y_r.at[n], yd(d))
        one.start()
        y_sends.append(one)

    def first(n, block, one):
        start(block.at[(y + 2) % YN, 0], one.at[0], 4 * n, 1)
        start(block.at[(y + 2) % YN, 1], one.at[1], 4 * n + 1, 3)

    def accumulate(dst, terms, rows):
        def some(r, carry):
            sl = pl.ds(pl.multiple_of(r * 32, 32), 32)
            total = terms[0][sl, :].astype(F32)
            for term in terms[1:]:
                total = total + term[sl, :].astype(F32)
            dst[sl, :] = total.astype(BF16)
            return carry

        lax.fori_loop(0, rows // 32, some, 0)

    def second(n, block, one, two, rows):
        for j, d in ((0, 1), (1, 3)):
            got(one.at[j], y_r.at[4 * n + j])
            mine = block.at[(y + d) % YN, j]
            accumulate(mine, [mine, one.at[j]], rows)
            start(block.at[(y + d) % YN], two.at[j], 4 * n + 2 + j, d)

    def last(n, block, two):
        for j in range(2):
            got(two.at[j], y_r.at[4 * n + 2 + j])

    def dec_grad(s, t):
        p = PAIR[s, t]
        for h in range(2):
            value = jnp.dot(coded_t[s], errs[2 * t + h].reshape(768, COLS), preferred_element_type=F32) * scale
            gdec[p, :, :, :, COLS * h:COLS * h + COLS] = value.astype(BF16).reshape(YN, 2, 32, COLS)
        first(p, gdec.at[p], rone_d.at[p])

    def dcoded(s):
        total_bias = jnp.zeros((1, FH), F32)
        for half in range(2):
            rows = slice(384 * half, 384 * half + 384)
            zs = slice(4 * half, 4 * half + 4)
            value = None
            for t in range(s, 2):
                for h in range(2):
                    term = lax.dot_general(errs[2 * t + h, zs].reshape(384, COLS), dw[PAIR[s, t], :, COLS * h:COLS * h + COLS],
                                           (((1,), (1,)), ((), ())), preferred_element_type=F32)
                    value = term if value is None else value + term
            grad = (value * gate[s, rows]).astype(BF16)
            dpre[s, rows] = grad
            total_bias = total_bias + jnp.sum(grad.astype(F32), axis=0, keepdims=True)
        bsum[s:s + 1, :] = total_bias * scale

    def enc_grad(s):
        for h in range(2):
            value = lax.dot_general(acts[2 * s + h].reshape(768, COLS), dpre[s], (((0,), (0,)), ((), ())), preferred_element_type=F32) * scale
            genc[s, :, h] = value.astype(BF16).reshape(YN, 288, FH)
        first(3 + s, genc.at[s], rone_e.at[s])

    dec_grad(0, 0)
    dcoded(1)
    enc_grad(1)
    dcoded(0)
    enc_grad(0)
    bsum[2:8, :] = jnp.zeros((6, FH), F32)
    b_sends = []
    for d in (1, 2, 3):
        one = rcopy(bsum, bland.at[d], b_s.at[d], b_r.at[d], yd(d))
        one.start()
        b_sends.append(one)
    second(0, gdec.at[0], rone_d.at[0], rtwo_d.at[0], 32)
    dec_grad(0, 1)
    second(4, genc.at[1], rone_e.at[1], rtwo_e.at[1], 288)
    dec_grad(1, 1)
    second(3, genc.at[0], rone_e.at[0], rtwo_e.at[0], 288)
    second(1, gdec.at[1], rone_d.at[1], rtwo_d.at[1], 32)
    second(2, gdec.at[2], rone_d.at[2], rtwo_d.at[2], 32)

    def dec_out(p):
        last(p, gdec.at[p], rtwo_d.at[p])
        for j in range(2):
            accumulate(gd_out.at[p, 32 * j:32 * j + 32], [gdec.at[p, y, j], rtwo_d.at[p, 0, j], rtwo_d.at[p, 1, j]], 32)

    def enc_out(s):
        last(3 + s, genc.at[s], rtwo_e.at[s])
        for j in range(2):
            mine = genc.at[s, y, j]
            accumulate(mine, [mine, rtwo_e.at[s, 0, j], rtwo_e.at[s, 1, j]], 288)
        one = rcopy(genc.at[s, y, 1 - xhi], swap.at[s], sw_s.at[s], sw_r.at[s], xd(2))
        one.start()
        return one

    dec_out(0)
    swaps = [enc_out(1), enc_out(0)]
    dec_out(1)
    dec_out(2)
    for d in (1, 2, 3):
        got(bland.at[d], b_r.at[d])
    gb_out[...] = bsum[...] + bland[1] + bland[2] + bland[3]
    for s in (1, 0):
        got(swap.at[s], sw_r.at[s])

        @pl.when(xhi == 0)
        def _():
            ge_out[s, :, :FH] = genc[s, y, 0]
            ge_out[s, :, FH:] = swap[s]

        @pl.when(xhi == 1)
        def _():
            ge_out[s, :, :FH] = swap[s]
            ge_out[s, :, FH:] = genc[s, y, 1]

    for one in sends + y_sends + b_sends + swaps:
        one.wait_send()


def shards(acts_in, targets, enc_weight, enc_bias, dec_weight):
    both = jnp.stack([acts_in, targets])
    both = both.reshape(2, TD, 4, COLS).transpose(0, 2, 1, 3)
    both = jnp.pad(both, ((0, 0), (0, 0), (0, 16 - TD), (0, 0)))
    dma = pltpu.SemaphoreType.DMA
    unit = (ROWS, COLS)
    vmem = pl.BlockSpec(memory_space=pltpu.VMEM)
    hbm = pl.BlockSpec(memory_space=pl.ANY)
    ge, gb, gd = pl.pallas_call(
        kernel,
        out_shape=(
            jax.ShapeDtypeStruct((2, 288, 512), BF16),
            jax.ShapeDtypeStruct((8, FH), F32),
            jax.ShapeDtypeStruct((3, 64, 2304), BF16),
        ),
        in_specs=[vmem, vmem, hbm, hbm],
        out_specs=(vmem, vmem, vmem),
        scratch_shapes=[
            pltpu.VMEM((2, XN, 16, COLS), BF16),
            pltpu.VMEM((XN, ZN, 2) + unit, BF16),
            pltpu.VMEM(unit, F32),
            pltpu.VMEM((XN, ZN, 2) + unit, BF16),
            pltpu.VMEM((2, 2304, FH), BF16),
            pltpu.VMEM((3, FH, 2304), BF16),
            pltpu.VMEM((2, 768, FH), F32),
            pltpu.VMEM((2, 768, FH), BF16),
            pltpu.VMEM((2, FH, 768), BF16),
            pltpu.VMEM((2, 768, FH), BF16),
            pltpu.VMEM((XN, ZN, 2) + unit, BF16),
            pltpu.VMEM((XN, ZN) + unit, BF16),
            pltpu.VMEM((36,) + unit, BF16),
            pltpu.VMEM((3, YN, 2, 32, 2304), BF16),
            pltpu.VMEM((2, YN, 2, 288, FH), BF16),
            pltpu.VMEM((3, 2, 32, 2304), BF16),
            pltpu.VMEM((2, 2, 288, FH), BF16),
            pltpu.VMEM((3, 2, 2, 32, 2304), BF16),
            pltpu.VMEM((2, 2, 2, 288, FH), BF16),
            pltpu.VMEM((2, 288, FH), BF16),
            pltpu.VMEM((8, FH), F32),
            pltpu.VMEM((4, 8, FH), F32),
            dma((2,)), dma((4,)), dma((4,)),
            dma((40,)), dma((40,)), dma((48,)), dma((48,)), dma((40,)), dma((40,)),
            dma((20,)), dma((20,)), dma((4,)), dma((4,)), dma((2,)), dma((2,)),
        ],
        compiler_params=pltpu.CompilerParams(collective_id=0, has_side_effects=True, vmem_limit_bytes=67_000_000),
    )(both, enc_bias, enc_weight, dec_weight)
    y = lax.axis_index("tok") % YN
    gb = lax.dynamic_slice(gb, (0, y * 64), (2, 64))
    return ge, gb, gd


def solution(mesh):
    return jax.shard_map(
        shards,
        mesh=mesh,
        in_specs=(
            P(("tok", "feat"), None, None),
            P(("tok", "feat"), None, None),
            P(None, None, "feat"),
            P(None, "feat"),
            P(None, "feat", None),
        ),
        out_specs=(
            P(None, "tok", "feat"),
            P(None, ("feat", "tok")),
            P(None, ("feat", "tok"), None),
        ),
        check_vma=False,
    )
```

time: 720 us -> 193 us (0.27)
  waiting for transfers between devices: 629 us -> 0 us
  Pallas kernels: 0 us -> 184 us
  matrix products: 30.2 us -> 0 us
  local copies, waits for them, and re-layouts: 29.1 us -> 8.01 us
  other arithmetic: 15.2 us -> 0.06 us
  between operations: 15 us -> 0.68 us
    psum x1 -> x0, waiting for transfers between devices: 233 us -> none  [shards(): lax.psum(jnp.stack(rebuilt, axis=1).astype(jnp.bfloat16), 'feat')]
    pallas_call x0 -> x1, Pallas kernels: none -> 184 us  [shards(): pl.pallas_call(kernel, out_shape=(jax.ShapeDtypeStruct((2, 288, 512), BF1...]
    unnamed x8 -> x0, waiting for transfers between devices: 169 us -> none
    all_gather x2 -> x0, waiting for transfers between devices: 118 us -> none  [the longest x1 70.8 us: shards(): lax.all_gather(acts_in, 'feat', axis=0, tiled=True)]
    reduce_scatter x1 -> x0, waiting for transfers between devices: 108 us -> none  [shards(): lax.psum_scatter(dec_terms.astype(jnp.bfloat16), 'tok', scatter_dimension...]
    dot_general x13 -> x0, matrix products: 30.2 us -> none  [the longest x2 6.86 us: shards(): lax.dot_general(errors[:, source, :], dec_weight[pair_slot(source, source...]
    another operation x6 -> x0, other arithmetic: 10.7 us -> none  [the longest x1 4.94 us: shards(): enc_terms = jnp.stack(enc_parts)]
    another operation x1 -> x4, local copies, waits for them, and re-layouts: 12.4 us -> 1.9 us  [shards(): both = jnp.stack([acts_in, targets])]
  transfers between devices with their start and end apart: 6 -> 0, of which waited for: 6 -> 0; matrix products, arithmetic and copies ran while one was open for 7% -> 0% of each run, Pallas kernels for 0% -> 0%
where the time goes in v1:
time: 193 us; the launch traced here: 192 us
  Pallas kernels  184 us (95%)
  local copies, waits for them, and re-layouts  8.01 us (4%)
    pallas_call x1, Pallas kernels, shards(): pl.pallas_call(kernel, out_shape=(jax.ShapeDtypeStruct((2, 288, 512), BF1...  184 us
    unnamed x2, local copies, waits for them, and re-layouts  4.05 us

profile of v1, /device:TPU:1, one launch (start us, length us, event | category | flops | bytes accessed | tf_op | source)
XLA Modules:
  0.0 192.3 jit_solution(4037329227851305062)
XLA Ops:
  0.6 0.9 stack.9
  1.6 0.9 stack.10
  2.6 0.1 maximum_bitcast_fusion
  2.6 0.7 pad.4.inp
  3.4 183.5 %shard_map.76 = (bf16[2,288,512]{2,1,0:T(8,128)(2,1)}, f32[8,256]{1,0:T(8,128)}, bf16[3,64,2304]{2,1,0:T(8,128)(2,1)}) custom-call(bf16[2,4,16,1152]{3,2,1,0:T(8,128)(2,1)} %pad.4.inp, f32[2,512]{1,0:T(2,128)} %eb.1, bf16[2,2304,512]{2,1,0:T(8,128)(2,1)} %ew_hbm.1, bf16[3,512,2304]{2,1,0:T(8,128)(2,1)} %dw_hbm.1), custom_call_target="tpu_custom_call" | custom-call | tf_op jit(solution)/shard_map/pallas_call | solution.py:458
  186.9 1.3 constant_dynamic-slice_fusion
  188.2 1.9 copy.12
  190.2 2.1 %copy.13 = bf16[3,64,2304]{2,1,0:T(8,128)(2,1)} copy(bf16[3,64,2304]{2,1,0:T(8,128)(2,1)} %get-tuple-element.14) | data formatting | bytes 1769472
  (2 shorter events, 0.0 us)

commit v2 on v1

v2 whole, which is shorter than its diff:
```python
import math

import jax
import jax.numpy as jnp
from jax import lax
from jax.experimental import pallas as pl
from jax.experimental.pallas import tpu as pltpu
from jax.sharding import PartitionSpec as P

MESH = pl.DeviceIdType.MESH
F32 = jnp.float32
BF16 = jnp.bfloat16
XN, ZN, YN = 4, 8, 4
TD = 12
ROWS = XN * TD
COLS = 1152
MAIN, REST = 512, 128
BASE = (0, MAIN + REST)
FH = 256
AG_ORDER = (0, -1, 1, -2, 2, -3, 3, 4)
RS_ORDER = (4, 3, -3, 2, -2, 1, -1, 0)
AG_INDEX = {s: i for i, s in enumerate(AG_ORDER)}
LATE = 3
PAIR = {(0, 0): 0, (0, 1): 1, (1, 1): 2}


def kernel(inp, eb, ew_hbm, dw_hbm, ge_out, gb_out, gd_out,
           land, acts, tgt, errs, ew, dw, gate, coded, coded_t, dpre, part, sib, recv,
           gdec, genc, rone_d, rone_e, rtwo_d, rtwo_e, swap, bsum, bland,
           wsem, a2a_s, a2a_r, ring_s, ring_r, y_s, y_r, b_s, b_r, sw_s, sw_r):
    fi = lax.axis_index("feat")
    ti = lax.axis_index("tok")
    core = fi % 2
    z = (fi // 2) % ZN
    xlo = fi // (2 * ZN)
    y = ti % YN
    xhi = ti // YN
    x = 2 * xhi + xlo
    scale = 1.0 / math.sqrt(3072.0)

    def dev(xx, zz, yy, cc):
        return ((xx % 2) * (2 * ZN) + zz * 2 + cc, (xx // 2) * YN + yy)

    def xd(d):
        return dev((x + d) % XN, z, y, core)

    def zd(d):
        return dev(x, (z + d + ZN) % ZN, y, core)

    def yd(d):
        return dev(x, z, (y + d) % YN, core)

    def zat(s):
        return (z + s + ZN) % ZN

    def xat(d):
        return (x + d) % XN

    sibling = dev(x, z, y, 1 - core)

    def rcopy(src, dst, ssem, rsem, device):
        return pltpu.make_async_remote_copy(src_ref=src, dst_ref=dst, send_sem=ssem, recv_sem=rsem, device_id=device, device_id_type=MESH)

    def got(dst, rsem):
        rcopy(dst, dst, rsem, rsem, sibling).wait_recv()

    bsum[...] = jnp.zeros_like(bsum)
    fo = pl.multiple_of(xhi * FH, FH)
    w_copies = [pltpu.make_async_copy(ew_hbm.at[:, :, pl.ds(fo, FH)], ew, wsem.at[0]),
                pltpu.make_async_copy(dw_hbm.at[:, pl.ds(fo, FH), :], dw, wsem.at[1])]
    for copy in w_copies:
        copy.start()

    barrier = pltpu.get_barrier_semaphore()
    partners = [sibling] + [xd(d) for d in (1, 2, 3)] + [zd(1), zd(-1)] + [yd(d) for d in (1, 2, 3)]
    for partner in partners:
        pl.semaphore_signal(barrier, inc=1, device_id=partner, device_id_type=MESH)
    pl.semaphore_wait(barrier, len(partners))

    sends = []
    for d in (1, 2, 3):
        send = rcopy(inp.at[:, xat(d)], land.at[:, d], a2a_s.at[d], a2a_r.at[d], xd(d))
        send.start()
        sends.append(send)
    land[:, 0] = inp[:, x]
    row = lax.broadcasted_iota(jnp.int32, (ROWS, XN * 16), 0)
    col = lax.broadcasted_iota(jnp.int32, (ROWS, XN * 16), 1)
    source = (x + XN - col // 16) % XN
    place = jnp.where((row == TD * source + col % 16) & (col % 16 < TD), 1.0, 0.0).astype(BF16)
    for d in (1, 2, 3):
        got(land.at[:, d], a2a_r.at[d])
    acts[x, z, core] = jnp.dot(place, land[0].reshape(XN * 16, COLS), preferred_element_type=F32).astype(BF16)
    tgt[...] = jnp.dot(place, land[1].reshape(XN * 16, COLS), preferred_element_type=F32)

    done = []

    def each(zero, one):
        pl.when(core == 0)(zero)
        pl.when(core == 1)(one)

    sent = ([], [])

    def gather(buf, lo, hi, stage):
        ss, rr = ring_s.at[stage], ring_r.at[stage]
        count = [0, 0]

        def send(c, ref, like, r, device):
            rcopy(ref, ref, ss.at[count[c]], rr.at[r], device).start()
            sent[c].append((like, ring_s, (stage, count[c])))
            count[c] += 1

        def like_unit():
            return buf.at[0, 0, 0, :, lo:hi]

        def like_bundle():
            return buf.at[:, 0, 0, :, lo:hi]


        def unit(c, xx, s):
            return buf.at[xx, zat(s), c, :, lo:hi]

        def bundle(c, s):
            return buf.at[:, zat(s), c, :, lo:hi]

        def to_x(i):
            s = AG_ORDER[i]
            send(0, unit(0, x, s), like_unit, 8 + i, xd(1))
            send(0, unit(0, x, s), like_unit, 16 + i, xd(3))

        def from_x(i):
            s = AG_ORDER[i]
            got(unit(0, xat(3), s), rr.at[8 + i])
            if s % 2 == 0:
                send(0, unit(0, xat(3), s), like_unit, 24 + i, xd(1))
            got(unit(0, xat(1), s), rr.at[16 + i])
            if s % 2 == 1:
                send(0, unit(0, xat(1), s), like_unit, 24 + i, xd(3))

        def to_sibling(i):
            s = AG_ORDER[i]
            got(unit(0, xat(2), s), rr.at[24 + i])
            send(0, bundle(0, s), like_bundle, 36 + i, sibling)

        def zero(j):
            if j == 0:
                send(0, unit(0, x, 0), like_unit, AG_INDEX[-1], zd(1))
                send(0, unit(0, x, 0), like_unit, AG_INDEX[1], zd(-1))
                to_x(0)
            elif j < 8:
                s = AG_ORDER[j]
                got(unit(0, x, s), rr.at[j])
                if s < 0:
                    send(0, unit(0, x, s), like_unit, AG_INDEX[s - 1] if s > -3 else 7, zd(1))
                elif s < 3:
                    send(0, unit(0, x, s), like_unit, AG_INDEX[s + 1], zd(-1))
                to_x(j)
            if LATE <= j < LATE + 8:
                from_x(j - LATE)
            if 2 * LATE <= j < 2 * LATE + 8:
                to_sibling(j - 2 * LATE)

        def one(j):
            if j == 0:
                for d in (1, 2, 3):
                    send(1, unit(1, x, 0), like_unit, d, xd(d))
            elif j == 1:
                for d in (0, 1, 3, 2):
                    if d:
                        got(unit(1, xat(4 - d), 0), rr.at[d])
                    send(1, unit(1, xat(4 - d), 0), like_unit, 4 + d, zd(1))
                    send(1, unit(1, xat(4 - d), 0), like_unit, 20 + d, zd(-1))
                send(1, bundle(1, 0), like_bundle, 36, sibling)
            elif 2 <= j < 6:
                k = j - 1
                for d in (0, 1, 3, 2):
                    for sign, base in ((-1, 4), (1, 20)):
                        if k == 4 and (d < 2) != (sign < 0):
                            continue
                        part_ = unit(1, xat(4 - d), sign * k)
                        got(part_, rr.at[base + 4 * (k - 1) + d])
                        if k < 3 or (k == 3 and (d < 2) == (sign < 0)):
                            send(1, part_, like_unit, base + 4 * k + d, zd(-sign))
                send(1, bundle(1, -k), like_bundle, 36 + AG_INDEX.get(-k, 7), sibling)
                if k < 4:
                    send(1, bundle(1, k), like_bundle, 36 + AG_INDEX[k], sibling)

        for j in range(8 + 2 * LATE):
            each(lambda: zero(j), lambda: one(j))
            yield
        for i in range(8):
            got(buf.at[:, zat(AG_ORDER[i]), 1 - core, :, lo:hi], rr.at[36 + i])
        yield

    def halves(lo, hi, stage, group):
        ss, rr = ring_s.at[stage], ring_r.at[stage]
        for i in group:
            zz = zat(RS_ORDER[i])
            one = rcopy(part.at[:, zz, 1 - core, :, lo:hi], sib.at[:, zz, :, lo:hi], ss.at[44 + i], rr.at[36 + i], sibling)
            one.start()
            done.append(one)

    def total_of(terms):
        total = terms[0][...].astype(F32)
        for term in terms[1:]:
            total = total + term[...].astype(F32)
        return total

    def scatter(lo, hi, stage):
        ss, rr = ring_s.at[stage], ring_r.at[stage]
        count = [0, 0]

        def slot(r):
            return recv.at[r, :, lo:hi]

        def send(c, src, r, device):
            rcopy(src, slot(r), ss.at[count[c]], rr.at[r], device).start()
            sent[c].append((lambda: slot(0), ring_s, (stage, count[c])))
            count[c] += 1

        def mine(c, xx, s):
            return part.at[xx, zat(s), c, :, lo:hi]

        def theirs(xx, s):
            return sib.at[xx, zat(s), :, lo:hi]

        def add(dst, terms):
            dst[...] = total_of(terms).astype(BF16)

        def finish(c, terms):
            errs[x, z, c, :, lo:hi] = (total_of(terms) - tgt[:, lo:hi]).astype(BF16)

        def across(i):
            s = RS_ORDER[i]
            got(sib.at[:, zat(s), :, lo:hi], rr.at[36 + i])
            add(mine(0, xat(2), s), [mine(0, xat(2), s), theirs(xat(2), s)])
            send(0, mine(0, xat(2), s), i, xd(1) if s % 2 == 0 else xd(3))

        def beside(i):
            s = RS_ORDER[i]
            got(slot(i), rr.at[i])
            for d, base, parity in ((1, 8, 0), (3, 16, 1)):
                terms = [mine(0, xat(d), s), theirs(xat(d), s)]
                if s % 2 == parity:
                    terms.append(slot(i))
                add(mine(0, xat(d), s), terms)
                send(0, mine(0, xat(d), s), base + i, xd(d))

        def along(i):
            s = RS_ORDER[i]
            k = abs(s)
            got(slot(8 + i), rr.at[8 + i])
            got(slot(16 + i), rr.at[16 + i])
            terms = [mine(0, x, s), theirs(x, s), slot(8 + i), slot(16 + i)]
            if 0 <= s < 4:
                got(slot(24 + 3 - k), rr.at[24 + 3 - k])
                terms.append(slot(24 + 3 - k))
            if -3 < s <= 0:
                got(slot(28 + 3 - k), rr.at[28 + 3 - k])
                terms.append(slot(28 + 3 - k))
            if s == 0:
                finish(0, terms)
                return
            add(mine(0, x, s), terms)
            if s > 0:
                send(0, mine(0, x, s), 24 + 4 - k, zd(1))
            else:
                send(0, mine(0, x, s), 28 + 4 - k, zd(-1))

        def zero(j):
            if j < 8:
                across(j)
            if LATE <= j < LATE + 8:
                beside(j - LATE)
            if 2 * LATE <= j < 2 * LATE + 8:
                along(j - 2 * LATE)

        def one(j):
            if j < 8:
                s = RS_ORDER[j]
                k = abs(s)
                got(sib.at[:, zat(s), :, lo:hi], rr.at[36 + j])
                for d in (2, 1, 3, 0):
                    xx = xat(d)
                    terms = [mine(1, xx, s), theirs(xx, s)]
                    for here, base in ((0 <= s < 4 and (k < 3 or d < 2), 0), (-4 < s <= 0 and (k < 3 or d >= 2), 16)):
                        if here:
                            got(slot(base + 4 * k + d), rr.at[base + 4 * k + d])
                            terms.append(slot(base + 4 * k + d))
                    add(mine(1, xx, s), terms)
                    if s == 4:
                        send(1, mine(1, xx, s), (0 if d < 2 else 16) + 12 + d, zd(1) if d < 2 else zd(-1))
                    elif s > 0:
                        send(1, mine(1, xx, s), 4 * (k - 1) + d, zd(1))
                    elif s < 0:
                        send(1, mine(1, xx, s), 16 + 4 * (k - 1) + d, zd(-1))
                    elif d:
                        send(1, mine(1, xx, s), 32 + d, xd(d))
            elif j == 7 + 2 * LATE:
                terms = [mine(1, x, 0)]
                for d in (1, 2, 3):
                    got(slot(32 + d), rr.at[32 + d])
                    terms.append(slot(32 + d))
                finish(1, terms)

        for j in range(8 + 2 * LATE):
            each(lambda: zero(j), lambda: one(j))
            yield

    def pieces(buf, layer, zs):
        lo = BASE[layer]
        rows = 768 if zs == slice(0, 8) else 384
        for xx in range(4):
            yield buf[xx, zs, :, :, lo:lo + MAIN].reshape(rows, MAIN), MAIN * xx
        rest = [buf[2 * layer + j, zs, :, :, MAIN:MAIN + REST].reshape(rows, REST) for j in range(2)]
        yield jnp.concatenate(rest, axis=1), 4 * MAIN

    bias = jnp.where(xhi == 0, eb[:, :FH], eb[:, FH:])

    def encode(s, half):
        rows = slice(384 * half, 384 * half + 384)
        zs = slice(4 * half, 4 * half + 4)
        value = bias[s:s + 1]
        for cols, first in pieces(acts, s, zs):
            value = value + jnp.dot(cols, ew[s, first:first + cols.shape[1]], preferred_element_type=F32)
        active = jnp.maximum(value, 0.0)
        gate[s, rows] = active
        code = (0.5 * active * active).astype(BF16)
        coded[s, zs] = code.reshape(4, 96, FH)
        coded_t[s, :, rows] = code.T

    def decode(t, xx, group):
        width = MAIN if xx < 4 else 2 * REST
        total = None
        for s in range(t + 1):
            codes = jnp.concatenate([coded[s, zat(RS_ORDER[i])] for i in group], axis=0)
            term = jnp.dot(codes, dw[PAIR[s, t], :, MAIN * xx:MAIN * xx + width], preferred_element_type=F32)
            total = term if total is None else total + term
        total = total.astype(BF16)
        for n, i in enumerate(group):
            rows = total[96 * n:96 * n + 96]
            zz = zat(RS_ORDER[i])
            if xx < 4:
                part[xx, zz, :, :, BASE[t]:BASE[t] + MAIN] = rows.reshape(2, ROWS, MAIN)
            else:
                for j in range(2):
                    part[2 * t + j, zz, :, :, MAIN:MAIN + REST] = rows[:, REST * j:REST * j + REST].reshape(2, ROWS, REST)

    def start(src, dst, n, d):
        one = rcopy(src, dst, y_s.at[n], y_r.at[n], yd(d))
        one.start()
        done.append(one)

    def first(n, block, one):
        start(block.at[(y + 2) % YN, 0], one.at[0], 4 * n, 1)
        start(block.at[(y + 2) % YN, 1], one.at[1], 4 * n + 1, 3)

    def accumulate(dst, terms, rows):
        def some(r, carry):
            sl = pl.ds(pl.multiple_of(r * 32, 32), 32)
            total = terms[0][sl, :].astype(F32)
            for term in terms[1:]:
                total = total + term[sl, :].astype(F32)
            dst[sl, :] = total.astype(BF16)
            return carry

        lax.fori_loop(0, rows // 32, some, 0)

    def second(n, block, one, two, rows):
        for j, d in ((0, 1), (1, 3)):
            got(one.at[j], y_r.at[4 * n + j])
            mine = block.at[(y + d) % YN, j]
            accumulate(mine, [mine, one.at[j]], rows)
            start(block.at[(y + d) % YN], two.at[j], 4 * n + 2 + j, d)

    def last(n, two):
        for j in range(2):
            got(two.at[j], y_r.at[4 * n + 2 + j])

    whole = slice(0, 8)

    def dec_grad(s, t):
        p = PAIR[s, t]
        for cols, at in pieces(errs, t, whole):
            width = cols.shape[1]
            value = jnp.dot(coded_t[s], cols, preferred_element_type=F32) * scale
            gdec[p, :, :, :, at:at + width] = value.astype(BF16).reshape(YN, 2, 32, width)
        first(p, gdec.at[p], rone_d.at[p])

    def dcoded(s):
        total_bias = jnp.zeros((1, FH), F32)
        for half in range(2):
            rows = slice(384 * half, 384 * half + 384)
            value = None
            for t in range(s, 2):
                for cols, at in pieces(errs, t, slice(4 * half, 4 * half + 4)):
                    term = lax.dot_general(cols, dw[PAIR[s, t], :, at:at + cols.shape[1]],
                                           (((1,), (1,)), ((), ())), preferred_element_type=F32)
                    value = term if value is None else value + term
            grad = (value * gate[s, rows]).astype(BF16)
            dpre[s, rows] = grad
            total_bias = total_bias + jnp.sum(grad.astype(F32), axis=0, keepdims=True)
        bsum[s:s + 1, :] = total_bias * scale

    def enc_grad(s):
        for cols, at in pieces(acts, s, whole):
            value = lax.dot_general(cols, dpre[s], (((0,), (0,)), ((), ())), preferred_element_type=F32) * scale
            value = value.astype(BF16)
            row, end = at, at + cols.shape[1]
            while row < end:
                stop = min(end, (row // 288 + 1) * 288)
                owner, place_ = row // 288, row % 288
                genc[s, owner % YN, owner // YN, place_:place_ + stop - row] = value[row - at:stop - at]
                row = stop
        first(3 + s, genc.at[s], rone_e.at[s])

    def dec_second(p):
        second(p, gdec.at[p], rone_d.at[p], rtwo_d.at[p], 32)

    def enc_second(s):
        second(3 + s, genc.at[s], rone_e.at[s], rtwo_e.at[s], 288)

    def dec_out(p):
        last(p, rtwo_d.at[p])
        for j in range(2):
            accumulate(gd_out.at[p, 32 * j:32 * j + 32], [gdec.at[p, y, j], rtwo_d.at[p, 0, j], rtwo_d.at[p, 1, j]], 32)

    def enc_out(s):
        last(3 + s, rtwo_e.at[s])
        for j in range(2):
            mine = genc.at[s, y, j]
            accumulate(mine, [mine, rtwo_e.at[s, 0, j], rtwo_e.at[s, 1, j]], 288)
        one = rcopy(genc.at[s, y, 1 - xhi], swap.at[s], sw_s.at[s], sw_r.at[s], xd(2))
        one.start()
        done.append(one)

    def turn(*steps):
        more = [next(one, "end") is None for one in steps]
        return more[0]

    inputs = gather(acts, 0, COLS, 0)
    while turn(inputs):
        pass
    for copy in w_copies:
        copy.wait()
    for s in range(2):
        for half in range(2):
            encode(s, half)
    one, zero = (MAIN, COLS), (0, MAIN)
    for group in (range(4), range(4, 8)):
        for xx in range(5):
            decode(1, xx, group)
        decode(0, 4, group)
        halves(*one, 1, group)
    for group in (range(4), range(4, 8)):
        for xx in range(4):
            decode(0, xx, group)
        halves(*zero, 2, group)
    early = scatter(*one, 1)
    while turn(early):
        pass
    early, late = gather(errs, *one, 3), scatter(*zero, 2)
    while turn(early, late):
        pass
    while turn(late):
        pass
    later = gather(errs, *zero, 4)
    turn(later)
    dec_grad(0, 1)
    turn(later)
    dec_grad(1, 1)
    turn(later)
    dec_second(1)
    turn(later)
    dec_second(2)
    turn(later)
    dcoded(1)
    turn(later)
    enc_grad(1)
    turn(later)
    turn(later)
    turn(later)
    enc_second(1)
    while turn(later):
        pass
    dcoded(0)
    enc_grad(0)
    dec_grad(0, 0)
    for d in (1, 2, 3):
        one = rcopy(bsum, bland.at[d], b_s.at[d], b_r.at[d], yd(d))
        one.start()
        done.append(one)
    enc_second(0)
    dec_second(0)
    dec_out(1)
    dec_out(2)
    enc_out(1)
    enc_out(0)
    for d in (1, 2, 3):
        got(bland.at[d], b_r.at[d])
    total = bsum[...] + bland[1] + bland[2] + bland[3]
    own = jnp.where(y == 0, total[:, :64], 0.0)
    for n in range(1, YN):
        own = own + jnp.where(y == n, total[:, 64 * n:64 * n + 64], 0.0)
    gb_out[...] = own[:2]
    dec_out(0)
    for s in (1, 0):
        got(swap.at[s], sw_r.at[s])

        @pl.when(xhi == 0)
        def _():
            ge_out[s, :, :FH] = genc[s, y, 0]
            ge_out[s, :, FH:] = swap[s]

        @pl.when(xhi == 1)
        def _():
            ge_out[s, :, :FH] = swap[s]
            ge_out[s, :, FH:] = genc[s, y, 1]

    for one in sends + done:
        one.wait_send()

    def drain(c):
        for like, sems, at in sent[c]:
            rcopy(like(), like(), sems.at[at], sems.at[at], sibling).wait_send()

    each(lambda: drain(0), lambda: drain(1))


def shards(acts_in, targets, enc_weight, enc_bias, dec_weight):
    both = jnp.stack([acts_in, targets])
    main = both[..., :4 * MAIN].reshape(2, TD, 2, 4, MAIN)
    rest = both[..., 4 * MAIN:].reshape(2, TD, 4, REST)
    both = jnp.concatenate([main[:, :, 0], rest, main[:, :, 1]], axis=-1).transpose(0, 2, 1, 3)
    both = jnp.pad(both, ((0, 0), (0, 0), (0, 16 - TD), (0, 0)))
    dma = pltpu.SemaphoreType.DMA
    unit = (ROWS, COLS)
    vmem = pl.BlockSpec(memory_space=pltpu.VMEM)
    hbm = pl.BlockSpec(memory_space=pl.ANY)
    ge, gb, gd = pl.pallas_call(
        kernel,
        out_shape=(
            jax.ShapeDtypeStruct((2, 288, 512), BF16),
            jax.ShapeDtypeStruct((2, 64), F32),
            jax.ShapeDtypeStruct((3, 64, 2304), BF16),
        ),
        in_specs=[vmem, vmem, hbm, hbm],
        out_specs=(vmem, vmem, vmem),
        scratch_shapes=[
            pltpu.VMEM((2, XN, 16, COLS), BF16),
            pltpu.VMEM((XN, ZN, 2) + unit, BF16),
            pltpu.VMEM(unit, F32),
            pltpu.VMEM((XN, ZN, 2) + unit, BF16),
            pltpu.VMEM((2, 2304, FH), BF16),
            pltpu.VMEM((3, FH, 2304), BF16),
            pltpu.VMEM((2, 768, FH), F32),
            pltpu.VMEM((2, ZN, 96, FH), BF16),
            pltpu.VMEM((2, FH, 768), BF16),
            pltpu.VMEM((2, 768, FH), BF16),
            pltpu.VMEM((XN, ZN, 2) + unit, BF16),
            pltpu.VMEM((XN, ZN) + unit, BF16),
            pltpu.VMEM((36,) + unit, BF16),
            pltpu.VMEM((3, YN, 2, 32, 2304), BF16),
            pltpu.VMEM((2, YN, 2, 288, FH), BF16),
            pltpu.VMEM((3, 2, 32, 2304), BF16),
            pltpu.VMEM((2, 2, 288, FH), BF16),
            pltpu.VMEM((3, 2, 2, 32, 2304), BF16),
            pltpu.VMEM((2, 2, 2, 288, FH), BF16),
            pltpu.VMEM((2, 288, FH), BF16),
            pltpu.VMEM((8, FH), F32),
            pltpu.VMEM((4, 8, FH), F32),
            dma((2,)), dma((4,)), dma((4,)),
            dma((5, 52)), dma((5, 44)),
            dma((20,)), dma((20,)), dma((4,)), dma((4,)), dma((2,)), dma((2,)),
        ],
        compiler_params=pltpu.CompilerParams(collective_id=0, has_side_effects=True, vmem_limit_bytes=67_000_000),
    )(both, enc_bias, enc_weight, dec_weight)
    return ge, gb, gd


def solution(mesh):
    return jax.shard_map(
        shards,
        mesh=mesh,
        in_specs=(
            P(("tok", "feat"), None, None),
            P(("tok", "feat"), None, None),
            P(None, None, "feat"),
            P(None, "feat"),
            P(None, "feat", None),
        ),
        out_specs=(
            P(None, "tok", "feat"),
            P(None, ("feat", "tok")),
            P(None, ("feat", "tok"), None),
        ),
        check_vma=False,
    )
```

time: 193 us -> 172 us (0.89)
  Pallas kernels: 184 us -> 163 us
  other arithmetic: 0.06 us -> 2.02 us
    pallas_call x1, Pallas kernels: 184 us -> 163 us  [shards(): pl.pallas_call(kernel, out_shape=(jax.ShapeDtypeStruct((2, 288, 512), BF1...]
    another operation x0 -> x2, other arithmetic: none -> 1.99 us  [shards(): both = jnp.stack([acts_in, targets])]
    unnamed x2 -> x3, local copies, waits for them, and re-layouts: 4.05 us -> 5.27 us
where the time goes in v2:
time: 172 us
  Pallas kernels  163 us (95%)
  local copies, waits for them, and re-layouts  6.28 us (4%)
  other arithmetic  2.02 us (1%)
    pallas_call x1, Pallas kernels, shards(): pl.pallas_call(kernel, out_shape=(jax.ShapeDtypeStruct((2, 288, 512), BF1...  163 us
    unnamed x3, local copies, waits for them, and re-layouts  5.27 us

profile of v2, /device:TPU:1, one launch (start us, length us, event | category | flops | bytes accessed | tf_op | source)
XLA Modules:
  0.0 171.6 jit_solution(10653293539712669043)
XLA Ops:
  0.6 0.8 pad_maximum_fusion
  1.4 1.2 fusion
  2.7 0.1 reshape.12
  2.8 0.1 fusion.1
  3.0 0.7 pad.4.inp
  3.7 162.6 %shard_map.76 = (bf16[2,288,512]{2,1,0:T(8,128)(2,1)}, f32[2,64]{1,0:T(2,128)}, bf16[3,64,2304]{2,1,0:T(8,128)(2,1)}) custom-call(bf16[2,4,16,1152]{3,2,1,0:T(8,128)(2,1)} %pad.4.inp, f32[2,512]{1,0:T(2,128)} %eb.1, bf16[2,2304,512]{2,1,0:T(8,128)(2,1)} %ew_hbm.1, bf16[3,512,2304]{2,1,0:T(8,128)(2,1)} %dw_hbm.1), custom_call_target="tpu_custom_call" | custom-call | tf_op jit(solution)/shard_map/pallas_call | solution.py:539
  166.3 1.9 %copy.18 = bf16[2,288,512]{2,1,0:T(8,128)(2,1)} copy(bf16[2,288,512]{2,1,0:T(8,128)(2,1)} %get-tuple-element.10) | data formatting | bytes 1179648
  168.2 1.2 copy.19
  169.4 2.1 %copy.20 = bf16[3,64,2304]{2,1,0:T(8,128)(2,1)} copy(bf16[3,64,2304]{2,1,0:T(8,128)(2,1)} %get-tuple-element.12) | data formatting | bytes 1769472
  (4 shorter events, 0.1 us)

commit v3 on v2

--- a/solution.py
+++ b/solution.py
@@ -72,7 +72,7 @@
         copy.start()
 
     barrier = pltpu.get_barrier_semaphore()
-    partners = [sibling] + [xd(d) for d in (1, 2, 3)] + [zd(1), zd(-1)] + [yd(d) for d in (1, 2, 3)]
+    partners = [sibling] + [xd(d) for d in (1, 2, 3)] + [zd(d) for d in (1, -1, 2, -2)] + [yd(d) for d in (1, 2, 3)]
     for partner in partners:
         pl.semaphore_signal(barrier, inc=1, device_id=partner, device_id_type=MESH)
     pl.semaphore_wait(barrier, len(partners))
@@ -123,41 +123,27 @@
             return buf.at[:, zat(s), c, :, lo:hi]
 
         def to_x(i):
-            s = AG_ORDER[i]
-            send(0, unit(0, x, s), like_unit, 8 + i, xd(1))
-            send(0, unit(0, x, s), like_unit, 16 + i, xd(3))
-
-        def from_x(i):
-            s = AG_ORDER[i]
-            got(unit(0, xat(3), s), rr.at[8 + i])
-            if s % 2 == 0:
-                send(0, unit(0, xat(3), s), like_unit, 24 + i, xd(1))
-            got(unit(0, xat(1), s), rr.at[16 + i])
-            if s % 2 == 1:
-                send(0, unit(0, xat(1), s), like_unit, 24 + i, xd(3))
+            for d, base in ((2, 24), (1, 8), (3, 16)):
+                send(0, unit(0, x, AG_ORDER[i]), like_unit, base + i, xd(d))
 
         def to_sibling(i):
             s = AG_ORDER[i]
-            got(unit(0, xat(2), s), rr.at[24 + i])
+            for d, base in ((3, 8), (1, 16), (2, 24)):
+                got(unit(0, xat(d), s), rr.at[base + i])
             send(0, bundle(0, s), like_bundle, 36 + i, sibling)
 
+        onward = {0: ((-1, 1), (1, -1), (-2, 2), (2, -2)), -2: ((-3, 1),), 2: ((3, -1), (4, -2))}
+
         def zero(j):
-            if j == 0:
-                send(0, unit(0, x, 0), like_unit, AG_INDEX[-1], zd(1))
-                send(0, unit(0, x, 0), like_unit, AG_INDEX[1], zd(-1))
-                to_x(0)
-            elif j < 8:
+            if j < 8:
                 s = AG_ORDER[j]
-                got(unit(0, x, s), rr.at[j])
-                if s < 0:
-                    send(0, unit(0, x, s), like_unit, AG_INDEX[s - 1] if s > -3 else 7, zd(1))
-                elif s < 3:
-                    send(0, unit(0, x, s), like_unit, AG_INDEX[s + 1], zd(-1))
+                if j:
+                    got(unit(0, x, s), rr.at[j])
+                for seen, d in onward.get(s, ()):
+                    send(0, unit(0, x, s), like_unit, AG_INDEX[seen], zd(d))
                 to_x(j)
             if LATE <= j < LATE + 8:
-                from_x(j - LATE)
-            if 2 * LATE <= j < 2 * LATE + 8:
-                to_sibling(j - 2 * LATE)
+                to_sibling(j - LATE)
 
         def one(j):
             if j == 0:
@@ -184,7 +170,7 @@
                 if k < 4:
                     send(1, bundle(1, k), like_bundle, 36 + AG_INDEX[k], sibling)
 
-        for j in range(8 + 2 * LATE):
+        for j in range(8 + LATE):
             each(lambda: zero(j), lambda: one(j))
             yield
         for i in range(8):
@@ -232,47 +218,31 @@
         def across(i):
             s = RS_ORDER[i]
             got(sib.at[:, zat(s), :, lo:hi], rr.at[36 + i])
-            add(mine(0, xat(2), s), [mine(0, xat(2), s), theirs(xat(2), s)])
-            send(0, mine(0, xat(2), s), i, xd(1) if s % 2 == 0 else xd(3))
-
-        def beside(i):
-            s = RS_ORDER[i]
-            got(slot(i), rr.at[i])
-            for d, base, parity in ((1, 8, 0), (3, 16, 1)):
-                terms = [mine(0, xat(d), s), theirs(xat(d), s)]
-                if s % 2 == parity:
-                    terms.append(slot(i))
-                add(mine(0, xat(d), s), terms)
-                send(0, mine(0, xat(d), s), base + i, xd(d))
+            for d in (2, 1, 3):
+                add(mine(0, xat(d), s), [mine(0, xat(d), s), theirs(xat(d), s)])
+                send(0, mine(0, xat(d), s), 8 * (d - 1) + i, xd(d))
+
+        passes = {4: (-2, 26, ()), 3: (1, 24, ()), -3: (-1, 25, ()), 2: (2, 29, (24,)), -2: (-2, 30, (25, 26)),
+                  1: (1, 27, ()), -1: (-1, 28, ()), 0: (0, 0, (27, 28, 29, 30))}
 
         def along(i):
             s = RS_ORDER[i]
-            k = abs(s)
-            got(slot(8 + i), rr.at[8 + i])
-            got(slot(16 + i), rr.at[16 + i])
-            terms = [mine(0, x, s), theirs(x, s), slot(8 + i), slot(16 + i)]
-            if 0 <= s < 4:
-                got(slot(24 + 3 - k), rr.at[24 + 3 - k])
-                terms.append(slot(24 + 3 - k))
-            if -3 < s <= 0:
-                got(slot(28 + 3 - k), rr.at[28 + 3 - k])
-                terms.append(slot(28 + 3 - k))
+            terms = [mine(0, x, s), theirs(x, s)]
+            to, there, before = passes[s]
+            for r in (i, 8 + i, 16 + i) + before:
+                got(slot(r), rr.at[r])
+                terms.append(slot(r))
             if s == 0:
                 finish(0, terms)
-                return
-            add(mine(0, x, s), terms)
-            if s > 0:
-                send(0, mine(0, x, s), 24 + 4 - k, zd(1))
             else:
-                send(0, mine(0, x, s), 28 + 4 - k, zd(-1))
+                add(mine(0, x, s), terms)
+                send(0, mine(0, x, s), there, zd(to))
 
         def zero(j):
             if j < 8:
                 across(j)
             if LATE <= j < LATE + 8:
-                beside(j - LATE)
-            if 2 * LATE <= j < 2 * LATE + 8:
-                along(j - 2 * LATE)
+                along(j - LATE)
 
         def one(j):
             if j < 8:
@@ -295,14 +265,14 @@
                         send(1, mine(1, xx, s), 16 + 4 * (k - 1) + d, zd(-1))
                     elif d:
                         send(1, mine(1, xx, s), 32 + d, xd(d))
-            elif j == 7 + 2 * LATE:
+            elif j == 7 + LATE:
                 terms = [mine(1, x, 0)]
                 for d in (1, 2, 3):
                     got(slot(32 + d), rr.at[32 + d])
                     terms.append(slot(32 + d))
                 finish(1, terms)
 
-        for j in range(8 + 2 * LATE):
+        for j in range(8 + LATE):
             each(lambda: zero(j), lambda: one(j))
             yield
 

time: 172 us -> 165 us (0.959)
  Pallas kernels: 163 us -> 156 us
    pallas_call x1, Pallas kernels: 163 us -> 156 us  [shards(): pl.pallas_call(kernel, out_shape=(jax.ShapeDtypeStruct((2, 288, 512), BF1...]
where the time goes in v3:
time: 165 us
  Pallas kernels  156 us (95%)
  local copies, waits for them, and re-layouts  6.28 us (4%)
  other arithmetic  2.02 us (1%)
    pallas_call x1, Pallas kernels, shards(): pl.pallas_call(kernel, out_shape=(jax.ShapeDtypeStruct((2, 288, 512), BF1...  156 us
    unnamed x3, local copies, waits for them, and re-layouts  5.27 us

profile of v3, /device:TPU:1, one launch (start us, length us, event | category | flops | bytes accessed | tf_op | source)
XLA Modules:
  0.0 164.9 jit_solution(13950999867450946760)
XLA Ops:
  0.6 0.8 pad_maximum_fusion
  1.4 1.2 fusion
  2.7 0.1 reshape.12
  2.8 0.1 fusion.1
  3.0 0.7 pad.4.inp
  3.7 155.9 %shard_map.76 = (bf16[2,288,512]{2,1,0:T(8,128)(2,1)}, f32[2,64]{1,0:T(2,128)}, bf16[3,64,2304]{2,1,0:T(8,128)(2,1)}) custom-call(bf16[2,4,16,1152]{3,2,1,0:T(8,128)(2,1)} %pad.4.inp, f32[2,512]{1,0:T(2,128)} %eb.1, bf16[2,2304,512]{2,1,0:T(8,128)(2,1)} %ew_hbm.1, bf16[3,512,2304]{2,1,0:T(8,128)(2,1)} %dw_hbm.1), custom_call_target="tpu_custom_call" | custom-call | tf_op jit(solution)/shard_map/pallas_call | solution.py:509
  159.6 1.9 %copy.18 = bf16[2,288,512]{2,1,0:T(8,128)(2,1)} copy(bf16[2,288,512]{2,1,0:T(8,128)(2,1)} %get-tuple-element.10) | data formatting | bytes 1179648
  161.5 1.2 copy.19
  162.7 2.1 %copy.20 = bf16[3,64,2304]{2,1,0:T(8,128)(2,1)} copy(bf16[3,64,2304]{2,1,0:T(8,128)(2,1)} %get-tuple-element.12) | data formatting | bytes 1769472
  (4 shorter events, 0.1 us)
